TPU v7x, 256 devices: a whole 4x4x8 slice. The times are simulated.
256 devices in a mesh: seq: 16 (over z, core), rep: 16 (over x, y).
Axes of the slice: x: 4, y: 4, z: 8, core: 2. Of those that a mesh axis runs over, the one named last changes fastest.
Arguments:
- tokens: bfloat16 [65536, 1024], P(('rep', 'seq')), parts along dimension 0, may hold values from -16 to 16
- segments: int32 [65536], P(('rep', 'seq')), parts along dimension 0, may hold values from 0 to 3, never falling along the last dimension, each value on 1 to 2048 neighbouring positions
- qkv_weight: bfloat16 [1024, 3072], replicated, may hold values from -1 to 1
- out_weight: bfloat16 [1024, 1024], replicated, may hold values from -0.1875 to 0.1875
- out_bias: float32 [1024], replicated, may hold values from -3 to 3
- ln_gain: float32 [1024], replicated, may hold values from 0.1 to 1.9
- ln_bias: float32 [1024], replicated, may hold values from -3 to 3
Outputs:
- normed: bfloat16 [65536, 1024], P(('rep', 'seq')), parts along dimension 0
- kv_cache: bfloat16 [65536, 2048], P('rep', 'seq'), parts along dimension 0
There are 16 independent parts, one for each index of `rep`. A program takes and returns all parts, laid end to end along the dimension named above; an argument that names none is the same for every part. Nothing has to cross between parts.
Inputs may be any that keep to these rules, and one draw needn't show every extreme that they name: `segments`: each prompt is a contiguous run of 1 to 2048 tokens, numbers never falling, one prompt exactly 2048 tokens.
All inputs are finite; a program needn't handle non-finite values.
Results may differ from a plain program's by a relative error of at most 0.008.
Values may be sent and summed in bfloat16 or wider, within the bound.
A program may use at most 128 MiB of HBM per device.

v0:
```python
import math
import jax
import jax.numpy as jnp
from jax import lax
from jax.sharding import PartitionSpec as P

HEADS = 16
HEAD = 64


def shards(tokens, segments, qkv_weight, out_weight, out_bias, ln_gain, ln_bias):
    tok_rows, width = tokens.shape
    scale = 1.0 / math.sqrt(HEAD)
    all_seg = lax.all_gather(segments, "seq", axis=0, tiled=True)
    proj = jnp.dot(tokens, qkv_weight, preferred_element_type=jnp.float32).astype(jnp.bfloat16)
    grouped = proj.reshape(tok_rows, HEADS, 3, HEAD)
    key_value = grouped[:, :, 1:, :].reshape(tok_rows, 2 * width)
    kv_cache = lax.all_to_all(key_value, "seq", split_axis=1, concat_axis=0, tiled=True)
    queries = jnp.moveaxis(grouped[:, :, 0, :], 1, 0)
    piece = lax.all_gather(key_value, "seq", axis=0, tiled=True)
    top_now = jnp.full((HEADS, tok_rows), -1e30, jnp.float32)
    total_now = jnp.zeros((HEADS, tok_rows), jnp.float32)
    acc_now = jnp.zeros((HEADS, tok_rows, HEAD), jnp.float32)
    count_rows = piece.shape[0]
    kept = segments[:, None] == all_seg[None, :]
    split_piece = piece.reshape(count_rows, HEADS, 2, HEAD)
    keys = jnp.moveaxis(split_piece[:, :, 0, :], 1, 0)
    values = jnp.moveaxis(split_piece[:, :, 1, :], 1, 0)

    def per_head(items):
        query, key_h, value_h, top_h, total_h, acc_h = items
        score = jnp.dot(query, key_h.T, preferred_element_type=jnp.float32) * scale
        score = jnp.where(kept, score, -1e30)
        new_top = jnp.maximum(top_h, jnp.max(score, axis=1))
        weight = jnp.where(kept, jnp.exp(score - new_top[:, None]), 0.0)
        factor = jnp.exp(top_h - new_top)
        new_total = total_h * factor + jnp.sum(weight, axis=1)
        new_acc = acc_h * factor[:, None] + jnp.dot(
            weight.astype(jnp.bfloat16), value_h, preferred_element_type=jnp.float32
        )
        return (new_top, new_total, new_acc)

    top_all, total_all, acc_all = lax.map(
        per_head, (queries, keys, values, top_now, total_now, acc_now)
    )
    context = (acc_all / total_all[:, :, None]).astype(jnp.bfloat16)
    gathered_ctx = jnp.moveaxis(context, 0, 1).reshape(tok_rows, width)
    mixed = (
        jnp.dot(gathered_ctx, out_weight, preferred_element_type=jnp.float32)
        + out_bias
        + tokens.astype(jnp.float32)
    )
    mean = jnp.mean(mixed, axis=1, keepdims=True)
    centered = mixed - mean
    variance = jnp.mean(centered * centered, axis=1, keepdims=True)
    normed = centered / jnp.sqrt(variance + 1e-05) * ln_gain + ln_bias
    return (normed.astype(jnp.bfloat16), kv_cache)


def solution(mesh):
    in_specs = (P(("rep", "seq"), None), P(("rep", "seq")), P(), P(), P(), P(), P())
    out_specs = (P(("rep", "seq"), None), P("rep", "seq"))
    return jax.shard_map(shards, mesh=mesh, in_specs=in_specs, out_specs=out_specs, check_vma=False)
```

profile of v0, /device:TPU:1, one launch (start us, length us, event | category | flops | bytes accessed | tf_op | source)
XLA Modules:
  0.0 246.1 jit_solution(5084389880568863316)
XLA Ops:
  7.2 6.0 %convolution_convert_fusion = bf16[256,3072]{1,0:T(8,128)(2,1)} fusion(bf16[256,1024]{1,0:T(8,128)(2,1)} %param.9, bf16[1024,3072]{1,0:T(8,128)(2,1)} %param.11), kind=kOutput, calls=%fused_computation.24 | convolution fusion | flops 1611399168 | bytes 8388608 | tf_op jit(solution)/shard_map/dot_general | solution.py:15
  13.3 2.6 %copy.20 = bf16[256,3072]{0,1:T(8,128)(2,1)} copy(bf16[256,3072]{1,0:T(8,128)(2,1)} %convolution_convert_fusion) | data formatting | bytes 3145728 | tf_op jit(solution)/shard_map/convert_element_type | solution.py:15
  15.9 2.3 slice.17
  18.2 10.0 %all-to-all-start = ((bf16[256,16,128]{0,2,1:T(8,128)(2,1)}), bf16[256,16,128]{0,2,1:T(8,128)(2,1)S(1)}, u32[]{:S(2)}, u32[]{:S(2)}) async-start(bf16[256,16,128]{0,2,1:T(8,128)(2,1)} %bitcast.60), calls=%async_computation | async-start | bytes 2097152 | tf_op jit(solution)/shard_map/all_to_all | solution.py:18
  28.2 46.9 %all-gather = s32[16,1,256]{2,1,0:T(1,128)S(1)} all-gather(s32[1,1,256]{2,1,0:T(1,128)S(1)} %bitcast.68), channel_id=1, replica_groups=mesh['seq'=16,'rep'=16] {'seq'}, dimensions={0}, use_global_device_ids=true | all-gather | bytes 17408 | tf_op jit(solution)/shard_map/all_gather | solution.py:14
  78.3 64.8 %all-gather.3.cloned.1.call-done = bf16[4096,2048]{0,1:T(8,128)(2,1)} async-done(((bf16[256,2048]{0,1:T(8,128)(2,1)}), bf16[4096,2048]{0,1:T(8,128)(2,1)}) %all-gather.3.cloned.1.call-update) | async-done | bytes 16777232 | tf_op jit(solution)/shard_map/all_gather | solution.py:20
  143.1 11.8 %slice_bitcast_fusion = (bf16[16,4096,64]{1,2,0:T(8,128)(2,1)}, bf16[16,4096,64]{1,2,0:T(8,128)(2,1)}) fusion(bf16[4096,16,2,64]{0,3,2,1:T(8,128)(2,1)} %bitcast.58), kind=kLoop, calls=%fused_computation.22 | loop fusion | bytes 33554432 | tf_op jit(solution)/shard_map/transpose | solution.py:28
  154.9 81.0 %while.13 = (s32[]{:T(128)}, f32[16,256]{1,0:T(8,128)S(1)}, f32[16,256,64]{1,2,0:T(8,128)S(1)}, bf16[16,256,64]{1,2,0:T(8,128)(2,1)}, bf16[16,4096,64]{1,2,0:T(8...) while((s32[]{:T(128)}, f32[16,256]{1,0:T(8,128)S(1)}, ...), condition=%wide.region_3.4_spmd.clone, body=%wide.region_0.3_spmd.clone.sunk | while | flops 281035520 | bytes 13797481 | solution.py:43
  157.9 2.0 fusion.42
  163.0 2.0 fusion.42
  168.0 2.0 fusion.42
  170.1 2.0 fusion.40
  173.1 2.0 fusion.42
  175.2 2.0 fusion.40
  178.2 2.0 fusion.42
  183.2 2.0 fusion.42
  185.3 2.0 fusion.40
  188.3 2.0 fusion.42
  190.4 2.0 fusion.40
  193.3 2.0 fusion.42
  198.4 2.0 fusion.42
  200.5 2.0 fusion.40
  203.5 2.0 fusion.42
  205.5 2.0 fusion.40
  208.5 2.0 fusion.42
  213.6 2.0 fusion.42
  215.7 2.0 fusion.40
  218.7 2.0 fusion.42
  223.7 2.0 fusion.42
  225.8 2.0 fusion.40
  228.8 2.0 fusion.42
  233.8 2.0 fusion.42
  (97 shorter events, 39.2 us)
Async XLA Ops:
  7.2 228.9 %copy-start = (bf16[1024,1024]{1,0:T(8,128)(2,1)S(1)}, bf16[1024,1024]{1,0:T(8,128)(2,1)}, u32[]{:S(2)}) copy-start(bf16[1024,1024]{1,0:T(8,128)(2,1)} %param.12) | copy-start | bytes 6291460
  7.2 136.0 %all-gather.3.cloned.1.call-start = ((), (), s32[]{:S(2)}) async-start(), calls=%async_computation.1 | async-start | bytes 17825792 | tf_op jit(solution)/shard_map/all_gather | solution.py:20
  13.3 14.9 %copy-start.2 = (s32[256]{0:T(256)S(1)}, s32[256]{0:T(256)}, u32[]{:S(2)}) copy-start(s32[256]{0:T(256)} %param.10) | copy-start | bytes 3076
  18.2 58.8 %all-to-all-start = ((bf16[256,16,128]{0,2,1:T(8,128)(2,1)}), bf16[256,16,128]{0,2,1:T(8,128)(2,1)S(1)}, u32[]{:S(2)}, u32[]{:S(2)}) async-start(bf16[256,16,128]{0,2,1:T(8,128)(2,1)} %bitcast.60), calls=%async_computation | async-start | bytes 2097152 | tf_op jit(solution)/shard_map/all_to_all | solution.py:18
  143.1 11.8 %copy-start.1 = (f32[16,256,64]{1,2,0:T(8,128)S(1)}, f32[16,256,64]{1,2,0:T(8,128)}, u32[]{:S(2)}) copy-start(f32[16,256,64]{1,2,0:T(8,128)} %custom-call.1) | copy-start | bytes 3145732
  154.9 81.1 %copy-start.3 = (f32[1024]{0:T(1024)S(1)}, f32[1024]{0:T(1024)}, u32[]{:S(2)}) copy-start(f32[1024]{0:T(1024)} %param.13) | copy-start | bytes 12292
  235.9 2.3 copy-start.4
  235.9 2.3 copy-start.5
Sparse Core Ops, SparseCore 0:
  18.3 124.7 all-gather.2
where the time goes:
time: 248 us; the launch traced here: 246 us
  matrix products  71.4 us (29%)
  waiting for transfers between devices  64.8 us (26%)
  blocking collectives  46.9 us (19%)
  local copies, waits for them, and re-layouts  20.6 us (8%)
  other arithmetic  17.7 us (7%)
  between operations  14.1 us (6%)
  starting transfers between devices  10 us (4%)
    all_gather x1, waiting for transfers between devices, shards(): piece = lax.all_gather(key_value, 'seq', axis=0, tiled=True)  64.8 us
    all_gather x1, blocking collectives, shards(): all_seg = lax.all_gather(segments, 'seq', axis=0, tiled=True)  46.9 us
    dot_general x16, matrix products, per_head(): jnp.dot(weight.astype(jnp.bfloat16), value_h, preferred_element_type=jnp....  32.1 us
    dot_general x16, matrix products, per_head(): score = jnp.dot(query, key_h.T, preferred_element_type=jnp.float32) * scale  31.4 us
    reduce_sum x16, other arithmetic, per_head(): new_total = total_h * factor + jnp.sum(weight, axis=1)  16 us
    transpose x1, local copies, waits for them, and re-layouts, shards(): values = jnp.moveaxis(split_piece[:, :, 1, :], 1, 0)  11.8 us
    all_to_all x1, starting transfers between devices, shards(): lax.all_to_all(key_value, 'seq', split_axis=1, concat_axis=0, tiled=True)  9.98 us
    dot_general x1, matrix products, shards(): jnp.dot(tokens, qkv_weight, preferred_element_type=jnp.float32)  6.04 us
  transfers between devices with their start and end apart: 2, of which 1 were waited for; matrix products, arithmetic and copies ran while one was open for 1% of the time, Pallas kernels for 0%

commit v1 on v0

--- a/solution.py
+++ b/solution.py
@@ -8,6 +8,18 @@
 HEAD = 64
 
 
+def arrange_joints(bus_axis, local):
+    return jnp.concatenate(
+        lax.all_to_all(
+            jnp.stack(jnp.split(local, lax.axis_size(bus_axis), axis=1)),
+            bus_axis,
+            split_axis=0,
+            concat_axis=0,
+        ),
+        axis=0,
+    )
+
+
 def shards(tokens, segments, qkv_weight, out_weight, out_bias, ln_gain, ln_bias):
     tok_rows, width = tokens.shape
     scale = 1.0 / math.sqrt(HEAD)
@@ -15,7 +27,7 @@
     proj = jnp.dot(tokens, qkv_weight, preferred_element_type=jnp.float32).astype(jnp.bfloat16)
     grouped = proj.reshape(tok_rows, HEADS, 3, HEAD)
     key_value = grouped[:, :, 1:, :].reshape(tok_rows, 2 * width)
-    kv_cache = lax.all_to_all(key_value, "seq", split_axis=1, concat_axis=0, tiled=True)
+    kv_cache = arrange_joints("seq", key_value)
     queries = jnp.moveaxis(grouped[:, :, 0, :], 1, 0)
     piece = lax.all_gather(key_value, "seq", axis=0, tiled=True)
     top_now = jnp.full((HEADS, tok_rows), -1e30, jnp.float32)

time: 248 us -> 252 us (1.016)
  local copies, waits for them, and re-layouts: 20.6 us -> 44.2 us
  waiting for transfers between devices: 64.8 us -> 45.2 us
    unnamed x12 -> x27, local copies, waits for them, and re-layouts: 0.03 us -> 22.1 us
    all_gather x1, waiting for transfers between devices: 64.8 us -> 45.2 us  [shards(): piece = lax.all_gather(key_value, 'seq', axis=0, tiled=True)]
  transfers between devices with their start and end apart: 2 -> 2, of which waited for: 1 -> 1; matrix products, arithmetic and copies ran while one was open for 1% -> 11% of each run, Pallas kernels for 0% -> 0%
where the time goes in v1:
time: 252 us; the launch traced here: 250 us
  matrix products  71.4 us (28%)
  blocking collectives  46.5 us (18%)
  waiting for transfers between devices  45.2 us (18%)
  local copies, waits for them, and re-layouts  44.2 us (18%)
  other arithmetic  17.7 us (7%)
  between operations  14.1 us (6%)
  starting transfers between devices  9.98 us (4%)
    all_gather x1, blocking collectives, shards(): all_seg = lax.all_gather(segments, 'seq', axis=0, tiled=True)  46.5 us
    all_gather x1, waiting for transfers between devices, shards(): piece = lax.all_gather(key_value, 'seq', axis=0, tiled=True)  45.2 us
    dot_general x16, matrix products, per_head(): jnp.dot(weight.astype(jnp.bfloat16), value_h, preferred_element_type=jnp....  32.1 us
    dot_general x16, matrix products, per_head(): score = jnp.dot(query, key_h.T, preferred_element_type=jnp.float32) * scale  31.4 us
    unnamed x27, local copies, waits for them, and re-layouts  22.1 us
    reduce_sum x16, other arithmetic, per_head(): new_total = total_h * factor + jnp.sum(weight, axis=1)  16 us
    transpose x1, local copies, waits for them, and re-layouts, shards(): values = jnp.moveaxis(split_piece[:, :, 1, :], 1, 0)  11.8 us
    all_to_all x1, starting transfers between devices, arrange_joints(): lax.all_to_all(jnp.stack(jnp.split(local, lax.axis_size(bus_axis), axis=1...  9.95 us
  transfers between devices with their start and end apart: 2, of which 1 were waited for; matrix products, arithmetic and copies ran while one was open for 11% of the time, Pallas kernels for 0%

profile of v1, /device:TPU:1, one launch (start us, length us, event | category | flops | bytes accessed | tf_op | source)
XLA Modules:
  0.0 249.7 jit_solution(1339144221076870435)
XLA Ops:
  7.2 6.0 %convolution_convert_fusion = bf16[256,3072]{1,0:T(8,128)(2,1)} fusion(bf16[256,1024]{1,0:T(8,128)(2,1)} %param.9, bf16[1024,3072]{1,0:T(8,128)(2,1)} %param.11), kind=kOutput, calls=%fused_computation.24 | convolution fusion | flops 1611399168 | bytes 8388608 | tf_op jit(solution)/shard_map/dot_general | solution.py:27
  13.3 2.6 %copy.19 = bf16[256,3072]{0,1:T(8,128)(2,1)} copy(bf16[256,3072]{1,0:T(8,128)(2,1)} %convolution_convert_fusion) | data formatting | bytes 3145728 | tf_op jit(solution)/shard_map/convert_element_type | solution.py:27
  15.9 2.3 slice.17
  41.8 9.9 %all-to-all-start = ((bf16[16,256,128]{1,2,0:T(8,128)(2,1)}), bf16[16,256,128]{1,2,0:T(8,128)(2,1)S(1)}, u32[]{:S(2)}, u32[]{:S(2)}) async-start(bf16[16,256,128]{1,2,0:T(8,128)(2,1)} %fusion.27), calls=%async_computation | async-start | bytes 2097152 | tf_op jit(solution)/shard_map/all_to_all | solution.py:13
  51.8 46.5 %all-gather = s32[16,1,256]{2,1,0:T(1,128)S(1)} all-gather(s32[1,1,256]{2,1,0:T(1,128)S(1)} %bitcast.144), channel_id=1, replica_groups=mesh['seq'=16,'rep'=16] {'seq'}, dimensions={0}, use_global_device_ids=true | all-gather | bytes 17408 | tf_op jit(solution)/shard_map/all_gather | solution.py:26
  101.5 45.2 %all-gather.3.cloned.1.call-done = bf16[4096,2048]{0,1:T(8,128)(2,1)} async-done(((bf16[256,2048]{0,1:T(8,128)(2,1)}), bf16[4096,2048]{0,1:T(8,128)(2,1)}) %all-gather.3.cloned.1.call-update) | async-done | bytes 16777232 | tf_op jit(solution)/shard_map/all_gather | solution.py:32
  146.7 11.8 %slice_bitcast_fusion = (bf16[16,4096,64]{1,2,0:T(8,128)(2,1)}, bf16[16,4096,64]{1,2,0:T(8,128)(2,1)}) fusion(bf16[4096,16,2,64]{0,3,2,1:T(8,128)(2,1)} %bitcast.120), kind=kLoop, calls=%fused_computation.22 | loop fusion | bytes 33554432 | tf_op jit(solution)/shard_map/transpose | solution.py:40
  158.5 81.0 %while.13 = (s32[]{:T(128)}, f32[16,256]{1,0:T(8,128)S(1)}, f32[16,256,64]{1,2,0:T(8,128)S(1)}, bf16[16,256,64]{1,2,0:T(8,128)(2,1)}, bf16[16,4096,64]{1,2,0:T(8...) while((s32[]{:T(128)}, f32[16,256]{1,0:T(8,128)S(1)}, ...), condition=%wide.region_3.4_spmd.clone, body=%wide.region_0.3_spmd.clone.sunk | while | flops 281035520 | bytes 13797481 | solution.py:55
  161.5 2.0 fusion.58
  163.6 2.0 fusion.56
  166.5 2.0 fusion.58
  168.6 2.0 fusion.56
  171.6 2.0 fusion.58
  176.7 2.0 fusion.58
  178.7 2.0 fusion.56
  181.7 2.0 fusion.58
  183.8 2.0 fusion.56
  186.8 2.0 fusion.58
  191.8 2.0 fusion.58
  193.9 2.0 fusion.56
  196.9 2.0 fusion.58
  202.0 2.0 fusion.58
  204.0 2.0 fusion.56
  207.0 2.0 fusion.58
  209.1 2.0 fusion.56
  212.1 2.0 fusion.58
  217.1 2.0 fusion.58
  219.2 2.0 fusion.56
  222.2 2.0 fusion.58
  227.3 2.0 fusion.58
  232.3 2.0 fusion.58
  237.4 2.0 fusion.58
  (113 shorter events, 62.8 us)
Async XLA Ops:
  7.2 232.4 %copy-start = (bf16[1024,1024]{1,0:T(8,128)(2,1)S(1)}, bf16[1024,1024]{1,0:T(8,128)(2,1)}, u32[]{:S(2)}) copy-start(bf16[1024,1024]{1,0:T(8,128)(2,1)} %param.12) | copy-start | bytes 6291460
  7.2 139.5 %all-gather.3.cloned.1.call-start = ((), (), s32[]{:S(2)}) async-start(), calls=%async_computation.1 | async-start | bytes 17825792 | tf_op jit(solution)/shard_map/all_gather | solution.py:32
  15.9 35.9 %copy-start.2 = (s32[256]{0:T(256)S(1)}, s32[256]{0:T(256)}, u32[]{:S(2)}) copy-start(s32[256]{0:T(256)} %param.10) | copy-start | bytes 3076
  41.8 58.4 %all-to-all-start = ((bf16[16,256,128]{1,2,0:T(8,128)(2,1)}), bf16[16,256,128]{1,2,0:T(8,128)(2,1)S(1)}, u32[]{:S(2)}, u32[]{:S(2)}) async-start(bf16[16,256,128]{1,2,0:T(8,128)(2,1)} %fusion.27), calls=%async_computation | async-start | bytes 2097152 | tf_op jit(solution)/shard_map/all_to_all | solution.py:13
  146.7 11.8 %copy-start.1 = (f32[16,256,64]{1,2,0:T(8,128)S(1)}, f32[16,256,64]{1,2,0:T(8,128)}, u32[]{:S(2)}) copy-start(f32[16,256,64]{1,2,0:T(8,128)} %custom-call.2) | copy-start | bytes 3145732
  158.5 81.1 %copy-start.3 = (f32[1024]{0:T(1024)S(1)}, f32[1024]{0:T(1024)}, u32[]{:S(2)}) copy-start(f32[1024]{0:T(1024)} %param.13) | copy-start | bytes 12292
  239.5 2.3 copy-start.4
  239.5 2.3 copy-start.5
Sparse Core Ops, SparseCore 0:
  18.3 128.3 all-gather.2
